TPU v7x, 32 devices: a whole 2x2x4 slice. The times are simulated.
32 devices in a mesh: groups: 2 (over y), seq: 4 (over z), dp: 4 (over x, core).
Axes of the slice: x: 2, y: 2, z: 4, core: 2. Of those that a mesh axis runs over, the one named last changes fastest.
Arguments:
- scan_input: bfloat16 [8, 512, 2048], P(('groups', 'dp'), 'seq'), parts along dimension 0, may hold values from -6 to 6
- gate_input: bfloat16 [8, 512, 2048], P(('groups', 'dp'), 'seq'), parts along dimension 0, may hold values from -6 to 6
- bmat: bfloat16 [8, 512, 128], P(('groups', 'dp'), 'seq'), parts along dimension 0, may hold values from -6 to 6
- cmat: bfloat16 [8, 512, 128], P(('groups', 'dp'), 'seq'), parts along dimension 0, may hold values from -0.5 to 0.5
- dt_raw: float32 [8, 512, 64], P(('groups', 'dp'), 'seq'), parts along dimension 0, may hold values from -4 to 4
- a_log: float32 [64], replicated
- d_skip: float32 [64], replicated, may hold values from 0.5 to 1.5
- gain: float32 [2048], replicated, may hold values from 0.1 to 1.9
- spans: int32 [8, 8, 2], P(('groups', 'dp')), parts along dimension 0, may hold values from 0 to 512, as said below
- cot: bfloat16 [8, 512, 2048], P(('groups', 'dp'), 'seq'), parts along dimension 0, may hold values from -6 to 6
Outputs:
- grad_x: bfloat16 [8, 512, 2048], P(('groups', 'dp'), 'seq'), parts along dimension 0
- grad_b: bfloat16 [8, 512, 128], P(('groups', 'dp'), 'seq'), parts along dimension 0
- grad_c: bfloat16 [8, 512, 128], P(('groups', 'dp'), 'seq'), parts along dimension 0
- grad_dt: float32 [8, 512, 64], P(('groups', 'dp'), 'seq'), parts along dimension 0
- grad_alog: float32 [128], P('groups'), parts along dimension 0
- grad_skip: float32 [128], P('groups'), parts along dimension 0
- grad_gain: float32 [4096], P('groups'), parts along dimension 0
There are 2 independent parts, one for each index of `groups`. A program takes and returns all parts, laid end to end along the dimension named above; an argument that names none is the same for every part. Nothing has to cross between parts.
Inputs may be any that keep to these rules, and one draw needn't show every extreme that they name: For each sequence the 8 spans are in order and tile the positions: the first starts at 0, each ends (exclusive) where the next starts, the last ends at 512, none is empty.
All inputs are finite; a program needn't handle non-finite values.
Results may differ from a plain program's by a relative error of at most 0.001.
Values sent between devices are 32-bit elements; how exact they have to be, the bound alone decides.
A program may use at most 128 MiB of HBM per device.

v0:
```python
import jax
import jax.numpy as jnp
from jax import lax
from jax.sharding import PartitionSpec as P

EPS = 1e-05
HI = lax.Precision.HIGHEST


def entering(shard, axis, combine, identity, reverse):
    peers, position = (lax.axis_size(axis), lax.axis_index(axis))
    everything = jax.tree.map(lambda part: lax.all_gather(part, axis), shard)
    start = jax.tree.map(
        lambda part, zero: jnp.broadcast_to(jnp.asarray(zero, part.dtype), part.shape),
        shard,
        identity,
    )

    def step(k, before):
        at = peers - 1 - k if reverse else k
        reached = at > position if reverse else at < position
        new = combine(before, jax.tree.map(lambda part: part[at], everything))
        return jax.tree.map(lambda a, b: jnp.where(reached, a, b), new, before)

    return lax.fori_loop(0, peers, step, start)


def combine(earlier, later):
    return (earlier[0] * later[0], later[0][:, None, None] * earlier[1] + later[1])


def on_device(scan_input, gate_input, bmat, cmat, dt_raw, a_log, d_skip, gain, spans, cot):
    rows = scan_input.shape[1]
    width = scan_input.shape[2]
    heads = a_log.shape[0]
    hdim = width // heads
    offset = lax.axis_index("seq") * rows
    xs = scan_input[0].astype(jnp.float32).reshape(rows, heads, hdim)
    zs = gate_input[0].astype(jnp.float32)
    bs = bmat[0].astype(jnp.float32)
    cs = cmat[0].astype(jnp.float32)
    raw = dt_raw[0]
    where_at = offset + jnp.arange(rows)
    flags = jnp.any(where_at[:, None] == spans[0][None, :, 0], 1).astype(jnp.int32)
    segl = jnp.cumsum(flags)
    step_size = jax.nn.softplus(raw)
    rate = jnp.exp(a_log)
    la = -rate[None, :] * step_size
    cum = jnp.cumsum(la, 0)
    place = jnp.arange(rows)
    same = (place[:, None] >= place[None, :]) & (segl[:, None] == segl[None, :])
    lmat = jnp.exp(jnp.where(same[None], cum.T[:, :, None] - cum.T[:, None, :], -jnp.inf))
    gmat = jnp.dot(cs, bs.T, precision=HI)
    xdt = xs * step_size[:, :, None]
    win = jnp.where((segl == 0)[:, None], jnp.exp(cum), 0.0)
    wout = jnp.exp(jnp.where((segl == segl[-1])[:, None], cum[-1][None, :] - cum, -jnp.inf))
    ablk = jnp.where(segl[-1] == 0, jnp.exp(cum[-1]), 0.0)
    weighted = xdt * wout[:, :, None]
    hloc = jnp.einsum("jhp,jn->hpn", weighted, bs, precision=HI)
    empty = jnp.zeros_like(hloc)
    _, hin = entering((ablk, hloc), "seq", combine, (jnp.ones_like(ablk), empty), False)
    sweights = lmat * gmat[None]
    y_intra = jnp.einsum("hij,jhp->ihp", sweights, xdt, precision=HI)
    cproj = jnp.einsum("in,hpn->ihp", cs, hin, precision=HI)
    y = y_intra + win[:, :, None] * cproj + d_skip[None, :, None] * xs
    gate = jax.nn.silu(zs)
    gated = y.reshape(rows, width) * gate
    scale = lax.rsqrt(jnp.mean(gated * gated, 1, keepdims=True) + EPS)
    normed = gated * scale
    upstream = cot[0].astype(jnp.float32)
    part_gain = jnp.sum(upstream * normed, 0)
    dnorm = upstream * gain[None, :]
    dgated = scale * dnorm - normed * scale * jnp.mean(dnorm * normed, 1, keepdims=True)
    dy = (dgated * gate).reshape(rows, heads, hdim)
    part_skip = jnp.sum(dy * xs, (0, 2))
    grad_in = dy * d_skip[None, :, None]
    dxdt = jnp.einsum("hij,ihp->jhp", sweights, dy, precision=HI)
    dsw = jnp.einsum("ihp,jhp->hij", dy, xdt, precision=HI)
    dgm = jnp.sum(dsw * lmat, 0)
    qmat = dsw * sweights
    dcum = jnp.sum(qmat, 2).T - jnp.sum(qmat, 1).T
    grad_c = jnp.dot(dgm, bs, precision=HI)
    grad_b = jnp.dot(dgm.T, cs, precision=HI)
    dwin = jnp.sum(dy * cproj, 2)
    dcum = dcum + dwin * win
    wdy = dy * win[:, :, None]
    grad_c = grad_c + jnp.einsum("ihp,hpn->in", wdy, hin, precision=HI)
    dhin = jnp.einsum("ihp,in->hpn", wdy, cs, precision=HI)
    _, gend = entering((ablk, dhin), "seq", combine, (jnp.ones_like(ablk), empty), True)
    vproj = jnp.einsum("jn,hpn->jhp", bs, gend, precision=HI)
    dwout = jnp.sum(vproj * xdt, 2)
    dxdt = dxdt + vproj * wout[:, :, None]
    grad_b = grad_b + jnp.einsum("jhp,hpn->jn", weighted, gend, precision=HI)
    tail = dwout * wout
    dablk = jnp.sum(gend * hin, (1, 2))
    lastrow = (place == rows - 1)[:, None]
    dcum = dcum - tail + jnp.where(lastrow, (jnp.sum(tail, 0) + dablk * ablk)[None, :], 0.0)
    grad_in = grad_in + dxdt * step_size[:, :, None]
    dstep = jnp.sum(dxdt * xs, 2)
    dla = jnp.flip(jnp.cumsum(jnp.flip(dcum, 0), 0), 0)
    dstep = dstep - rate[None, :] * dla
    part_alog = jnp.sum(dla * la, 0)
    grad_dt = dstep * jax.nn.sigmoid(raw)
    grad_alog, grad_skip, grad_gain = lax.psum((part_alog, part_skip, part_gain), ("seq", "dp"))
    return (
        grad_in.reshape(rows, width).astype(jnp.bfloat16)[None],
        grad_b.astype(jnp.bfloat16)[None],
        grad_c.astype(jnp.bfloat16)[None],
        grad_dt[None],
        grad_alog,
        grad_skip,
        grad_gain,
    )


def solution(mesh):
    return jax.shard_map(
        on_device,
        mesh=mesh,
        in_specs=(
            P(("groups", "dp"), "seq", None),
            P(("groups", "dp"), "seq", None),
            P(("groups", "dp"), "seq", None),
            P(("groups", "dp"), "seq", None),
            P(("groups", "dp"), "seq", None),
            P(),
            P(),
            P(),
            P(("groups", "dp"), None, None),
            P(("groups", "dp"), "seq", None),
        ),
        out_specs=(
            P(("groups", "dp"), "seq", None),
            P(("groups", "dp"), "seq", None),
            P(("groups", "dp"), "seq", None),
            P(("groups", "dp"), "seq", None),
            P("groups"),
            P("groups"),
            P("groups"),
        ),
        check_vma=False,
    )
```

profile of v0, /device:TPU:0, one launch (start us, length us, event | category | flops | bytes accessed | tf_op | source)
XLA Modules:
  0.0 258.3 jit_solution(2906881014786928078)
XLA Ops:
  7.2 0.0 all-gather.6.cloned.1.call-start
  7.3 0.7 slice_bitcast_fusion
  8.0 0.1 compare_reduce_fusion
  8.1 0.1 copy.91
  8.2 0.2 broadcast_in_dim.97
  8.4 0.5 slice.15
  8.9 0.1 reduce.1
  9.0 1.2 fusion.89
  10.2 0.8 compare_select_fusion
  11.0 0.1 copy.92
  11.8 0.2 reduce_window_sum.24
  11.9 0.1 copy.95
  12.0 0.7 broadcast_compare_fusion.1
  12.7 1.3 copy.90
  14.0 0.1 exponential_select_fusion
  14.1 0.1 bitcast_multiply_fusion.3
  14.3 1.6 fusion.68
  15.8 0.0 all-gather.6.cloned.1.call-update
  15.9 0.0 all-gather.8.cloned.1.call-start
  15.9 0.7 copy.93
  16.6 1.2 copy.97
  17.9 1.2 copy.98
  19.1 0.1 mul.290
  19.2 12.6 %all-gather.2 = f32[4,1,64]{2,1,0:T(1,128)S(1)} all-gather(f32[1,1,64]{2,1,0:T(1,128)S(1)} %get-tuple-element.340), channel_id=1, replica_groups=mesh['groups'=2,'seq'=4,'dp'=4] {'seq'}, dimensions={0}, use_global_device_ids=true | all-gather | bytes 1280 | tf_op jit(solution)/shard_map/all_gather | solution.py:12
  31.8 0.1 fusion.62
  31.9 0.1 fusion.71
  32.1 67.4 %all-gather.6.cloned.1.call-done = f32[256,32,128]{2,1,0:T(8,128)} async-done(((f32[64,32,128]{2,1,0:T(8,128)}), f32[256,32,128]{2,1,0:T(8,128)}) %all-gather.6.cloned.1.call-update) | async-done | bytes 4194320 | tf_op jit(solution)/shard_map/all_gather | solution.py:12
  99.5 6.1 %while.30 = (s32[]{:T(128)}, f32[64,32,128]{2,1,0:T(8,128)S(1)}, s32[]{:T(128)}, f32[4,64]{1,0:T(4,128)S(1)}, f32[4,64,32,128]{3,2,1,0:T(8,128)}, /*index=5*/s32[]{:T(128)}, s32[]{:T(128)}) while((s32[]{:T(128)}, f32[64,32,128]{2,1,0:T(8,128)S(1)}, s32[]{:T(128)}, f32[4,64]{1,0:T(4,128)S(1)}, f32[4,64,32,128]{3,2,1,0:T(8,128)}, ...), condition=%wide.region_4.5_spmd.clone, body=%wide.region_3.4_spmd.clone.sunk | while | flops 1048580 | bytes 3146601 | solution.py:25
  99.5 1.5 fusion.104
  101.0 1.5 fusion.104
  102.6 1.5 fusion.104
  104.1 1.5 fusion.104
  105.6 0.6 convolution_bitcast_fusion.1
  106.2 8.4 %multiply_reduce_fusion.6 = (f32[128]{0:T(128)S(1)}, f32[128,64,32]{0,2,1:T(8,128)S(1)}) fusion(f32[128,64,32]{0,2,1:T(8,128)S(1)} %bitcast.171, f32[64]{0:T(128)S(1)} %copy-done.17, f32[128,64,32]{0,2,1:T(8,128)S(1)} %convolution_bitcast_fusion.1, f32[128,64]{0,1:T(8,128)S(1)} %get-tuple-element.343, f32[128,128]{1,0:T(8,128)S(1)} %fusion.71, ...), kind=kOutput, calls=%fused_computation.61 | convolution fusion | flops 409468800 | bytes 3851008 | tf_op jit(solution)/shard_map/hij,jhp->ihp/dot_general | solution.py:63
  114.6 1.4 copy.99
  116.0 2.2 fusion.46
  118.2 2.1 subtract_multiply_fusion
  120.3 1.6 fusion.49
  121.9 0.0 all-gather.8.cloned.1.call-update
  122.0 0.5 iota_compare_fusion.1
  122.5 1.8 convolution_bitcast_fusion.2
  124.3 10.8 %fusion.8 = (f32[64,128]{1,0:T(8,128)}, f32[64,128]{1,0:T(8,128)}, f32[128,128]{1,0:T(8,128)S(1)}) fusion(f32[128,128]{1,0:T(8,128)S(1)} %fusion.71, f32[64,128]{1,0:T(8,128)} %copy.93, pred[128,128]{1,0:T(8,128)(4,1)} %copy-done.13, f32[128,64,32]{0,2,1:T(8,128)S(1)} %subtract_multiply_fusion, f32[128,64]{0,1:T(8,128)S(1)} %get-tuple-element.345, ...), kind=kOutput, calls=%fused_computation.12 | convolution fusion | flops 411533312 | bytes 1851392 | tf_op jit(solution)/shard_map/ihp,jhp->hij/dot_general | solution.py:78
  135.2 0.8 fusion.37
  136.0 65.4 %all-gather.8.cloned.1.call-done = f32[256,32,128]{2,1,0:T(8,128)} async-done(((f32[64,32,128]{2,1,0:T(8,128)}), f32[256,32,128]{2,1,0:T(8,128)}) %all-gather.8.cloned.1.call-update) | async-done | bytes 4194320 | tf_op jit(solution)/shard_map/all_gather | solution.py:12
  201.4 6.1 %while.31 = (s32[]{:T(128)}, f32[64,32,128]{2,1,0:T(8,128)S(1)}, s32[]{:T(128)}, f32[4,64]{1,0:T(4,128)S(1)}, f32[4,64,32,128]{3,2,1,0:T(8,128)}, /*index=5*/s32[]{:T(128)}, s32[]{:T(128)}, s32[]{:T(128)}, s32[]{:T(128)}) while((s32[]{:T(128)}, f32[64,32,128]{2,1,0:T(8,128)S(1)}, s32[]{:T(128)}, f32[4,64]{1,0:T(4,128)S(1)}, ...), condition=%wide.region_8.9_spmd.clone, body=%wide.region_7.8_spmd.clone.sunk | while | flops 1048584 | bytes 3146663 | solution.py:25
  201.4 1.5 fusion.105
  202.9 1.5 fusion.105
  204.5 1.5 fusion.105
  206.0 1.5 fusion.105
  207.6 0.6 convolution_bitcast_fusion
  208.2 0.6 multiply_reduce_fusion.2
  208.8 1.9 convolution_bitcast_fusion.3
  210.7 4.9 %multiply_reduce_fusion.1 = (f32[64]{0:T(128)S(1)}, f32[128,64]{0,1:T(8,128)S(1)}, f32[128,64]{0,1:T(8,128)S(1)}, f32[128,64]{0,1:T(8,128)S(1)}, bf16[128,64,32]{0,2,1:T(8,128)(2,1)S(1)}) fusion(f32[128,64,32]{0,2,1:T(8,128)S(1)} %subtract_multiply_fusion, f32[128,64,32]{0,2,1:T(8,128)S(1)} %convolution_bitcast_fusion, ...), kind=kOutput, calls=%fused_computation.53 | convolution fusion | flops 409968576 | bytes 4473344 | tf_op jit(solution)/shard_map/hij,ihp->jhp/dot_general | solution.py:77
  215.6 0.1 multiply_reduce_fusion.8
  215.7 0.1 fusion.64
  215.8 0.1 rev.7
  215.9 0.1 copy.100
  216.0 0.2 reduce_window_sum.25
  216.2 0.1 copy.101
  216.2 0.1 rev.8
  216.3 0.9 fusion.38
  217.2 1.0 copy.102
  218.2 0.8 multiply_reduce_fusion.7
  219.0 32.4 %all-reduce = (f32[64]{0:T(128)}, f32[64]{0:T(128)}, f32[2048]{0:T(1024)}) all-reduce(f32[64]{0:T(128)S(1)} %get-tuple-element.341, f32[64]{0:T(128)S(1)} %get-tuple-element.311, f32[2048]{0:T(1024)S(1)} %get-tuple-element.309), channel_id=1, replica_groups=mesh['groups'=2,'seq'=4,'dp'=4] {'seq','dp'}, use_global_device_ids=true, to_apply=%region_19.20 | all-reduce | flops 2176 | bytes 17408 | tf_op jit(solution)/shard_map/psum | solution.py:104
  (54 shorter events, 0.2 us)
Async XLA Ops:
  7.2 7.1 %copy-start = (bf16[1,128,128]{2,1,0:T(8,128)(2,1)S(1)}, bf16[1,128,128]{2,1,0:T(8,128)(2,1)}, u32[]{:S(2)}) copy-start(bf16[1,128,128]{2,1,0:T(8,128)(2,1)} %param.16) | copy-start | bytes 98308
  7.2 10.7 %copy-start.4 = (bf16[1,128,2048]{2,1,0:T(8,128)(2,1)S(1)}, bf16[1,128,2048]{2,1,0:T(8,128)(2,1)}, u32[]{:S(2)}) copy-start(bf16[1,128,2048]{2,1,0:T(8,128)(2,1)} %param.23) | copy-start | bytes 1572868
  7.2 92.3 %all-gather.6.cloned.1.call-start = ((), (), s32[]{:S(2)}) async-start(), calls=%async_computation | async-start | bytes 5242880 | tf_op jit(solution)/shard_map/all_gather | solution.py:12
  14.0 85.5 %copy-start.2 = (bf16[1,128,2048]{1,2,0:T(8,128)(2,1)}, bf16[1,128,2048]{1,2,0:T(8,128)(2,1)S(1)}, u32[]{:S(2)}) copy-start(bf16[1,128,2048]{1,2,0:T(8,128)(2,1)S(1)} %copy.90) | copy-start | bytes 1572868
  14.0 5.1 %copy-start.9 = (f32[2048]{0:T(1024)S(1)}, f32[2048]{0:T(1024)}, u32[]{:S(2)}) copy-start(f32[2048]{0:T(1024)} %param.21) | copy-start | bytes 24580
  14.0 17.9 %copy-start.7 = (bf16[1,128,128]{2,1,0:T(8,128)(2,1)S(1)}, bf16[1,128,128]{2,1,0:T(8,128)(2,1)}, u32[]{:S(2)}) copy-start(bf16[1,128,128]{2,1,0:T(8,128)(2,1)} %param.17) | copy-start | bytes 98308
  15.9 185.5 %all-gather.8.cloned.1.call-start = ((), (), s32[]{:S(2)}) async-start(), calls=%async_computation.1 | async-start | bytes 5242880 | tf_op jit(solution)/shard_map/all_gather | solution.py:12
  31.9 74.3 %copy-start.13 = (pred[128,128]{1,0:T(8,128)(4,1)}, pred[128,128]{1,0:T(8,128)(4,1)S(1)}, u32[]{:S(2)}) copy-start(pred[128,128]{1,0:T(8,128)(4,1)S(1)} %fusion.62) | copy-start | bytes 49156
  99.5 6.7 %copy-start.17 = (f32[64]{0:T(128)S(1)}, f32[64]{0:T(128)}, u32[]{:S(2)}) copy-start(f32[64]{0:T(128)} %param.20) | copy-start | bytes 772
  106.2 8.4 %copy-start.5 = (f32[128,64,32]{0,2,1:T(8,128)}, f32[128,64,32]{0,2,1:T(8,128)S(1)}, u32[]{:S(2)}) copy-start(f32[128,64,32]{0,2,1:T(8,128)S(1)} %convolution_bitcast_fusion.1) | copy-start | bytes 3145732
  114.6 3.6 %copy-start.1 = (f32[128,64,32]{0,2,1:T(8,128)}, f32[128,64,32]{0,2,1:T(8,128)S(1)}, u32[]{:S(2)}) copy-start(f32[128,64,32]{0,2,1:T(8,128)S(1)} %get-tuple-element.352) | copy-start | bytes 3145732
  207.5 1.2 copy-start.3
  207.5 3.1 %copy-start.6 = (f32[128,64,32]{0,2,1:T(8,128)S(1)}, f32[128,64,32]{0,2,1:T(8,128)}, u32[]{:S(2)}) copy-start(f32[128,64,32]{0,2,1:T(8,128)} %copy-done.5) | copy-start | bytes 3145732
  207.5 3.1 %copy-start.10 = (f32[64,128]{1,0:T(8,128)S(1)}, f32[64,128]{1,0:T(8,128)}, u32[]{:S(2)}) copy-start(f32[64,128]{1,0:T(8,128)} %copy.93) | copy-start | bytes 98308
  207.6 3.1 %copy-start.14 = (pred[128,128]{1,0:T(8,128)(4,1)S(1)}, pred[128,128]{1,0:T(8,128)(4,1)}, u32[]{:S(2)}) copy-start(pred[128,128]{1,0:T(8,128)(4,1)} %copy-done.13) | copy-start | bytes 49156
  207.6 3.1 %copy-start.18 = (f32[64]{0:T(128)S(1)}, f32[64]{0:T(128)}, u32[]{:S(2)}) copy-start(f32[64]{0:T(128)} %param.20) | copy-start | bytes 772
  210.7 5.0 %copy-start.11 = (f32[64,128]{1,0:T(8,128)S(1)}, f32[64,128]{1,0:T(8,128)}, u32[]{:S(2)}) copy-start(f32[64,128]{1,0:T(8,128)} %get-tuple-element.306) | copy-start | bytes 98308
  210.7 5.0 %copy-start.12 = (f32[64,128]{1,0:T(8,128)S(1)}, f32[64,128]{1,0:T(8,128)}, u32[]{:S(2)}) copy-start(f32[64,128]{1,0:T(8,128)} %get-tuple-element.307) | copy-start | bytes 98308
  210.7 5.0 %copy-start.16 = (pred[128]{0:T(512)(128)(4,1)S(1)}, pred[128]{0:T(512)(128)(4,1)}, u32[]{:S(2)}) copy-start(pred[128]{0:T(512)(128)(4,1)} %iota_compare_fusion.1) | copy-start | bytes 388
  210.7 7.5 %copy-start.8 = (f32[1,128,64]{1,2,0:T(8,128)S(1)}, f32[1,128,64]{1,2,0:T(8,128)}, u32[]{:S(2)}) copy-start(f32[1,128,64]{1,2,0:T(8,128)} %param.18) | copy-start | bytes 98308
  210.7 7.5 %copy-start.15 = (f32[64]{0:T(128)S(1)}, f32[64]{0:T(128)}, u32[]{:S(2)}) copy-start(f32[64]{0:T(128)} %get-tuple-element.347) | copy-start | bytes 772
Sparse Core Ops, SparseCore 0:
  16.0 83.4 all-gather.5
  122.1 79.2 all-gather.7
where the time goes:
time: 259 us; the launch traced here: 258 us
  waiting for transfers between devices  133 us (51%)
  blocking collectives  45.1 us (17%)
  matrix products  34 us (13%)
  other arithmetic  21.9 us (8%)
  between operations  15.1 us (6%)
  local copies, waits for them, and re-layouts  8.92 us (3%)
    all_gather x2, waiting for transfers between devices, entering(): everything = jax.tree.map(lambda part: lax.all_gather(part, axis), shard)  133 us
    psum x1, blocking collectives, on_device(): lax.psum((part_alog, part_skip, part_gain), ('seq', 'dp'))  32.4 us
    all_gather x1, blocking collectives, entering(): everything = jax.tree.map(lambda part: lax.all_gather(part, axis), shard)  12.6 us
    select_n x8, other arithmetic, step(): return jax.tree.map(lambda a, b: jnp.where(reached, a, b), new, before)  11.9 us
    dot_general x1, matrix products, on_device(): dsw = jnp.einsum('ihp,jhp->hij', dy, xdt, precision=HI)  10.8 us
    dot_general x1, matrix products, on_device(): y_intra = jnp.einsum('hij,jhp->ihp', sweights, xdt, precision=HI)  8.38 us
  transfers between devices with their start and end apart: 2, of which 2 were waited for; matrix products, arithmetic and copies ran while one was open for 7% of the time, Pallas kernels for 0%

commit v1 on v0

--- a/solution.py
+++ b/solution.py
@@ -5,6 +5,7 @@
 
 EPS = 1e-05
 HI = lax.Precision.HIGHEST
+proceed_the_panel = lambda body: lax.psum(lax.psum(body, "dp"), axis_name="seq")
 
 
 def entering(shard, axis, combine, identity, reverse):
@@ -101,7 +102,7 @@
     dstep = dstep - rate[None, :] * dla
     part_alog = jnp.sum(dla * la, 0)
     grad_dt = dstep * jax.nn.sigmoid(raw)
-    grad_alog, grad_skip, grad_gain = lax.psum((part_alog, part_skip, part_gain), ("seq", "dp"))
+    grad_alog, grad_skip, grad_gain = proceed_the_panel((part_alog, part_skip, part_gain))
     return (
         grad_in.reshape(rows, width).astype(jnp.bfloat16)[None],
         grad_b.astype(jnp.bfloat16)[None],

time: 259 us -> 244 us (0.942)
  blocking collectives: 45.1 us -> 29.8 us
    psum x1 -> x2, blocking collectives: 32.4 us -> 17.2 us  [the longest x1 9.96 us: lax.psum(lax.psum(body, 'dp'), axis_name='seq')]
where the time goes in v1:
time: 244 us; the launch traced here: 243 us
  waiting for transfers between devices  133 us (55%)
  matrix products  34 us (14%)
  blocking collectives  29.8 us (12%)
  other arithmetic  21.9 us (9%)
  between operations  15.1 us (6%)
  local copies, waits for them, and re-layouts  8.92 us (4%)
    all_gather x2, waiting for transfers between devices, entering(): everything = jax.tree.map(lambda part: lax.all_gather(part, axis), shard)  133 us
    all_gather x1, blocking collectives, entering(): everything = jax.tree.map(lambda part: lax.all_gather(part, axis), shard)  12.6 us
    select_n x8, other arithmetic, step(): return jax.tree.map(lambda a, b: jnp.where(reached, a, b), new, before)  11.9 us
    dot_general x1, matrix products, on_device(): dsw = jnp.einsum('ihp,jhp->hij', dy, xdt, precision=HI)  10.8 us
    psum x1, blocking collectives, lax.psum(lax.psum(body, 'dp'), axis_name='seq')  9.96 us
    dot_general x1, matrix products, on_device(): y_intra = jnp.einsum('hij,jhp->ihp', sweights, xdt, precision=HI)  8.38 us
    psum x1, blocking collectives, lax.psum(body, 'dp')  7.22 us
  transfers between devices with their start and end apart: 2, of which 2 were waited for; matrix products, arithmetic and copies ran while one was open for 7% of the time, Pallas kernels for 0%

profile of v1, /device:TPU:0, one launch (start us, length us, event | category | flops | bytes accessed | tf_op | source)
XLA Modules:
  0.0 243.0 jit_solution(13497310739363138715)
XLA Ops:
  7.2 0.0 all-gather.6.cloned.1.call-start
  7.3 0.7 slice_bitcast_fusion
  8.0 0.1 compare_reduce_fusion
  8.1 0.1 copy.91
  8.2 0.2 broadcast_in_dim.97
  8.4 0.5 slice.15
  8.9 0.1 reduce.1
  9.0 1.2 fusion.89
  10.2 0.8 compare_select_fusion
  11.0 0.1 copy.92
  11.8 0.2 reduce_window_sum.24
  11.9 0.1 copy.95
  12.0 0.7 broadcast_compare_fusion.1
  12.7 1.3 copy.90
  14.0 0.1 exponential_select_fusion
  14.1 0.1 bitcast_multiply_fusion.3
  14.3 1.6 fusion.68
  15.8 0.0 all-gather.6.cloned.1.call-update
  15.9 0.0 all-gather.8.cloned.1.call-start
  15.9 0.7 copy.93
  16.6 1.2 copy.97
  17.9 1.2 copy.98
  19.1 0.1 mul.290
  19.2 12.6 %all-gather.2 = f32[4,1,64]{2,1,0:T(1,128)S(1)} all-gather(f32[1,1,64]{2,1,0:T(1,128)S(1)} %get-tuple-element.343), channel_id=1, replica_groups=mesh['groups'=2,'seq'=4,'dp'=4] {'seq'}, dimensions={0}, use_global_device_ids=true | all-gather | bytes 1280 | tf_op jit(solution)/shard_map/all_gather | solution.py:13
  31.8 0.1 fusion.62
  31.9 0.1 fusion.71
  32.1 67.4 %all-gather.6.cloned.1.call-done = f32[256,32,128]{2,1,0:T(8,128)} async-done(((f32[64,32,128]{2,1,0:T(8,128)}), f32[256,32,128]{2,1,0:T(8,128)}) %all-gather.6.cloned.1.call-update) | async-done | bytes 4194320 | tf_op jit(solution)/shard_map/all_gather | solution.py:13
  99.5 6.1 %while.30 = (s32[]{:T(128)}, f32[64,32,128]{2,1,0:T(8,128)S(1)}, s32[]{:T(128)}, f32[4,64]{1,0:T(4,128)S(1)}, f32[4,64,32,128]{3,2,1,0:T(8,128)}, /*index=5*/s32[]{:T(128)}, s32[]{:T(128)}) while((s32[]{:T(128)}, f32[64,32,128]{2,1,0:T(8,128)S(1)}, s32[]{:T(128)}, f32[4,64]{1,0:T(4,128)S(1)}, f32[4,64,32,128]{3,2,1,0:T(8,128)}, ...), condition=%wide.region_4.5_spmd.clone, body=%wide.region_3.4_spmd.clone.sunk | while | flops 1048580 | bytes 3146601 | solution.py:26
  99.5 1.5 fusion.104
  101.0 1.5 fusion.104
  102.6 1.5 fusion.104
  104.1 1.5 fusion.104
  105.6 0.6 convolution_bitcast_fusion.1
  106.2 8.4 %multiply_reduce_fusion.6 = (f32[128]{0:T(128)S(1)}, f32[128,64,32]{0,2,1:T(8,128)S(1)}) fusion(f32[128,64,32]{0,2,1:T(8,128)S(1)} %bitcast.171, f32[64]{0:T(128)S(1)} %copy-done.17, f32[128,64,32]{0,2,1:T(8,128)S(1)} %convolution_bitcast_fusion.1, f32[128,64]{0,1:T(8,128)S(1)} %get-tuple-element.346, f32[128,128]{1,0:T(8,128)S(1)} %fusion.71, ...), kind=kOutput, calls=%fused_computation.61 | convolution fusion | flops 409468800 | bytes 3851008 | tf_op jit(solution)/shard_map/hij,jhp->ihp/dot_general | solution.py:64
  114.6 1.4 copy.99
  116.0 2.2 fusion.46
  118.2 2.1 subtract_multiply_fusion
  120.3 1.6 fusion.49
  122.0 0.5 iota_compare_fusion.1
  122.5 1.8 convolution_bitcast_fusion.2
  124.3 10.8 %fusion.8 = (f32[64,128]{1,0:T(8,128)}, f32[64,128]{1,0:T(8,128)}, f32[128,128]{1,0:T(8,128)S(1)}) fusion(f32[128,128]{1,0:T(8,128)S(1)} %fusion.71, f32[64,128]{1,0:T(8,128)} %copy.93, pred[128,128]{1,0:T(8,128)(4,1)} %copy-done.13, f32[128,64,32]{0,2,1:T(8,128)S(1)} %subtract_multiply_fusion, f32[128,64]{0,1:T(8,128)S(1)} %get-tuple-element.348, ...), kind=kOutput, calls=%fused_computation.12 | convolution fusion | flops 411533312 | bytes 1851392 | tf_op jit(solution)/shard_map/ihp,jhp->hij/dot_general | solution.py:79
  135.2 0.8 fusion.37
  136.0 65.4 %all-gather.8.cloned.1.call-done = f32[256,32,128]{2,1,0:T(8,128)} async-done(((f32[64,32,128]{2,1,0:T(8,128)}), f32[256,32,128]{2,1,0:T(8,128)}) %all-gather.8.cloned.1.call-update) | async-done | bytes 4194320 | tf_op jit(solution)/shard_map/all_gather | solution.py:13
  201.4 6.1 %while.31 = (s32[]{:T(128)}, f32[64,32,128]{2,1,0:T(8,128)S(1)}, s32[]{:T(128)}, f32[4,64]{1,0:T(4,128)S(1)}, f32[4,64,32,128]{3,2,1,0:T(8,128)}, /*index=5*/s32[]{:T(128)}, s32[]{:T(128)}, s32[]{:T(128)}, s32[]{:T(128)}) while((s32[]{:T(128)}, f32[64,32,128]{2,1,0:T(8,128)S(1)}, s32[]{:T(128)}, f32[4,64]{1,0:T(4,128)S(1)}, ...), condition=%wide.region_8.9_spmd.clone, body=%wide.region_7.8_spmd.clone.sunk | while | flops 1048584 | bytes 3146663 | solution.py:26
  201.4 1.5 fusion.105
  202.9 1.5 fusion.105
  204.5 1.5 fusion.105
  206.0 1.5 fusion.105
  207.6 0.6 convolution_bitcast_fusion
  208.2 0.6 multiply_reduce_fusion.2
  208.8 1.9 convolution_bitcast_fusion.3
  210.7 4.9 %multiply_reduce_fusion.1 = (f32[64]{0:T(128)S(1)}, f32[128,64]{0,1:T(8,128)S(1)}, f32[128,64]{0,1:T(8,128)S(1)}, f32[128,64]{0,1:T(8,128)S(1)}, bf16[128,64,32]{0,2,1:T(8,128)(2,1)S(1)}) fusion(f32[128,64,32]{0,2,1:T(8,128)S(1)} %subtract_multiply_fusion, f32[128,64,32]{0,2,1:T(8,128)S(1)} %convolution_bitcast_fusion, ...), kind=kOutput, calls=%fused_computation.53 | convolution fusion | flops 409968576 | bytes 4473344 | tf_op jit(solution)/shard_map/hij,ihp->jhp/dot_general | solution.py:78
  215.6 0.1 multiply_reduce_fusion.8
  215.7 0.1 fusion.64
  215.8 0.1 rev.7
  215.9 0.1 copy.100
  216.0 0.2 reduce_window_sum.25
  216.2 0.1 copy.101
  216.2 0.1 rev.8
  216.3 0.9 fusion.38
  217.2 1.0 copy.102
  218.2 0.8 multiply_reduce_fusion.7
  219.0 7.2 %all-reduce = (f32[64]{0:T(128)S(1)}, f32[64]{0:T(128)S(1)}, f32[2048]{0:T(1024)S(1)}) all-reduce(f32[64]{0:T(128)S(1)} %get-tuple-element.344, f32[64]{0:T(128)S(1)} %get-tuple-element.311, f32[2048]{0:T(1024)S(1)} %get-tuple-element.309), channel_id=1, replica_groups=mesh['groups'=2,'seq'=4,'dp'=4] {'dp'}, use_global_device_ids=true, to_apply=%region_19.20 | all-reduce | flops 2176 | bytes 17408 | tf_op jit(solution)/shard_map/psum | solution.py:8
  226.2 10.0 %all-reduce.1 = (f32[64]{0:T(128)}, f32[64]{0:T(128)}, f32[2048]{0:T(1024)}) all-reduce(f32[64]{0:T(128)S(1)} %get-tuple-element.335, f32[64]{0:T(128)S(1)} %get-tuple-element.336, f32[2048]{0:T(1024)S(1)} %get-tuple-element.337), channel_id=1, replica_groups=mesh['groups'=2,'seq'=4,'dp'=4] {'seq'}, use_global_device_ids=true, to_apply=%region_20.21 | all-reduce | flops 2176 | bytes 17408 | tf_op jit(solution)/shard_map/psum | solution.py:8
  (55 shorter events, 0.2 us)
Async XLA Ops:
  7.2 7.1 %copy-start = (bf16[1,128,128]{2,1,0:T(8,128)(2,1)S(1)}, bf16[1,128,128]{2,1,0:T(8,128)(2,1)}, u32[]{:S(2)}) copy-start(bf16[1,128,128]{2,1,0:T(8,128)(2,1)} %param.16) | copy-start | bytes 98308
  7.2 10.7 %copy-start.4 = (bf16[1,128,2048]{2,1,0:T(8,128)(2,1)S(1)}, bf16[1,128,2048]{2,1,0:T(8,128)(2,1)}, u32[]{:S(2)}) copy-start(bf16[1,128,2048]{2,1,0:T(8,128)(2,1)} %param.23) | copy-start | bytes 1572868
  7.2 92.3 %all-gather.6.cloned.1.call-start = ((), (), s32[]{:S(2)}) async-start(), calls=%async_computation | async-start | bytes 5242880 | tf_op jit(solution)/shard_map/all_gather | solution.py:13
  14.0 85.5 %copy-start.2 = (bf16[1,128,2048]{1,2,0:T(8,128)(2,1)}, bf16[1,128,2048]{1,2,0:T(8,128)(2,1)S(1)}, u32[]{:S(2)}) copy-start(bf16[1,128,2048]{1,2,0:T(8,128)(2,1)S(1)} %copy.90) | copy-start | bytes 1572868
  14.0 5.1 %copy-start.9 = (f32[2048]{0:T(1024)S(1)}, f32[2048]{0:T(1024)}, u32[]{:S(2)}) copy-start(f32[2048]{0:T(1024)} %param.21) | copy-start | bytes 24580
  14.0 17.9 %copy-start.7 = (bf16[1,128,128]{2,1,0:T(8,128)(2,1)S(1)}, bf16[1,128,128]{2,1,0:T(8,128)(2,1)}, u32[]{:S(2)}) copy-start(bf16[1,128,128]{2,1,0:T(8,128)(2,1)} %param.17) | copy-start | bytes 98308
  15.9 185.5 %all-gather.8.cloned.1.call-start = ((), (), s32[]{:S(2)}) async-start(), calls=%async_computation.1 | async-start | bytes 5242880 | tf_op jit(solution)/shard_map/all_gather | solution.py:13
  31.9 74.3 %copy-start.13 = (pred[128,128]{1,0:T(8,128)(4,1)}, pred[128,128]{1,0:T(8,128)(4,1)S(1)}, u32[]{:S(2)}) copy-start(pred[128,128]{1,0:T(8,128)(4,1)S(1)} %fusion.62) | copy-start | bytes 49156
  99.5 6.7 %copy-start.17 = (f32[64]{0:T(128)S(1)}, f32[64]{0:T(128)}, u32[]{:S(2)}) copy-start(f32[64]{0:T(128)} %param.20) | copy-start | bytes 772
  106.2 8.4 %copy-start.5 = (f32[128,64,32]{0,2,1:T(8,128)}, f32[128,64,32]{0,2,1:T(8,128)S(1)}, u32[]{:S(2)}) copy-start(f32[128,64,32]{0,2,1:T(8,128)S(1)} %convolution_bitcast_fusion.1) | copy-start | bytes 3145732
  114.6 3.6 %copy-start.1 = (f32[128,64,32]{0,2,1:T(8,128)}, f32[128,64,32]{0,2,1:T(8,128)S(1)}, u32[]{:S(2)}) copy-start(f32[128,64,32]{0,2,1:T(8,128)S(1)} %get-tuple-element.355) | copy-start | bytes 3145732
  207.5 1.2 copy-start.3
  207.5 3.1 %copy-start.6 = (f32[128,64,32]{0,2,1:T(8,128)S(1)}, f32[128,64,32]{0,2,1:T(8,128)}, u32[]{:S(2)}) copy-start(f32[128,64,32]{0,2,1:T(8,128)} %copy-done.5) | copy-start | bytes 3145732
  207.5 3.1 %copy-start.10 = (f32[64,128]{1,0:T(8,128)S(1)}, f32[64,128]{1,0:T(8,128)}, u32[]{:S(2)}) copy-start(f32[64,128]{1,0:T(8,128)} %copy.93) | copy-start | bytes 98308
  207.6 3.1 %copy-start.14 = (pred[128,128]{1,0:T(8,128)(4,1)S(1)}, pred[128,128]{1,0:T(8,128)(4,1)}, u32[]{:S(2)}) copy-start(pred[128,128]{1,0:T(8,128)(4,1)} %copy-done.13) | copy-start | bytes 49156
  207.6 3.1 %copy-start.18 = (f32[64]{0:T(128)S(1)}, f32[64]{0:T(128)}, u32[]{:S(2)}) copy-start(f32[64]{0:T(128)} %param.20) | copy-start | bytes 772
  210.7 5.0 %copy-start.11 = (f32[64,128]{1,0:T(8,128)S(1)}, f32[64,128]{1,0:T(8,128)}, u32[]{:S(2)}) copy-start(f32[64,128]{1,0:T(8,128)} %get-tuple-element.306) | copy-start | bytes 98308
  210.7 5.0 %copy-start.12 = (f32[64,128]{1,0:T(8,128)S(1)}, f32[64,128]{1,0:T(8,128)}, u32[]{:S(2)}) copy-start(f32[64,128]{1,0:T(8,128)} %get-tuple-element.307) | copy-start | bytes 98308
  210.7 5.0 %copy-start.16 = (pred[128]{0:T(512)(128)(4,1)S(1)}, pred[128]{0:T(512)(128)(4,1)}, u32[]{:S(2)}) copy-start(pred[128]{0:T(512)(128)(4,1)} %iota_compare_fusion.1) | copy-start | bytes 388
  210.7 7.5 %copy-start.8 = (f32[1,128,64]{1,2,0:T(8,128)S(1)}, f32[1,128,64]{1,2,0:T(8,128)}, u32[]{:S(2)}) copy-start(f32[1,128,64]{1,2,0:T(8,128)} %param.18) | copy-start | bytes 98308
  210.7 7.5 %copy-start.15 = (f32[64]{0:T(128)S(1)}, f32[64]{0:T(128)}, u32[]{:S(2)}) copy-start(f32[64]{0:T(128)} %get-tuple-element.350) | copy-start | bytes 772
Sparse Core Ops, SparseCore 0:
  16.0 83.4 all-gather.5
  122.1 79.2 all-gather.7
